TPU v7x, 512 devices: a whole 4x8x8 slice. The times are simulated.
512 devices in a mesh: row: 16 (over z, core), col: 8 (over y_hi, x), depth: 4 (over y_lo).
Axes of the slice: x: 4, y: 8 (y_hi: 2, y_lo: 4; y = y_hi * 4 + y_lo), z: 8, core: 2. Of those that a mesh axis runs over, the one named last changes fastest.
Arguments:
- density: bfloat16 [8192, 8192], P('row', 'col'), as said below
Outputs:
- purified: float32 [8192, 8192], P('row', ('col', 'depth'))
Inputs may be any that keep to these rules, and one draw needn't show every extreme that they name: density is symmetric: density[i, j] == density[j, i] for every i and j, for any seed.
All inputs are finite; a program needn't handle non-finite values.
Results may differ from a plain program's by a relative error of at most 0.002.
Values may be sent and summed in bfloat16 or wider, within the bound.
A program may use at most 64 MiB of HBM per device.

v0:
```python
import jax
import jax.numpy as jnp
from jax import lax
from jax.sharding import PartitionSpec as P


def on_device(density):
    rows_blk, cols_blk = density.shape
    depth_n = lax.axis_size("depth")
    strip_len = rows_blk // depth_n
    groups = cols_blk // rows_blk
    layer_idx = lax.axis_index("depth")
    col_strips = lax.dynamic_index_in_dim(
        density.reshape(rows_blk, groups, depth_n, strip_len), layer_idx, 2, keepdims=False
    ).reshape(rows_blk, groups * strip_len)
    row_strips = lax.dynamic_index_in_dim(
        density.reshape(depth_n, strip_len, cols_blk), layer_idx, 0, keepdims=False
    )

    def gather_slab(local_slab):
        return lax.all_gather(local_slab, "col", axis=1, tiled=True)

    def multiply(left_full):
        return jnp.dot(
            left_full,
            lax.all_gather(row_strips, "row", axis=0, tiled=True),
            preferred_element_type=jnp.float32,
        )

    partial_square = multiply(gather_slab(col_strips))
    square = lax.psum(partial_square, "depth").astype(jnp.bfloat16)
    square_strips = lax.dynamic_index_in_dim(
        square.reshape(rows_blk, groups, depth_n, strip_len), layer_idx, 2, keepdims=False
    ).reshape(rows_blk, groups * strip_len)
    partial_cube = multiply(gather_slab(square_strips))
    cube_sum = lax.psum_scatter(-2.0 * partial_cube, "depth", scatter_dimension=1, tiled=True)
    share_width = cols_blk // depth_n
    own_square = lax.dynamic_slice_in_dim(square, layer_idx * share_width, share_width, 1).astype(
        jnp.float32
    )
    return cube_sum + 3.0 * own_square


def solution(mesh):
    placed = (P("row", "col"),)
    return jax.shard_map(
        on_device, mesh=mesh, in_specs=placed, out_specs=P("row", ("col", "depth")), check_vma=False
    )
```

profile of v0, /device:TPU:1, one launch (start us, length us, event | category | flops | bytes accessed | tf_op | source)
XLA Modules:
  0.0 366.3 jit_solution(4787188095062731809)
XLA Ops:
  6.5 0.0 all-gather.5.cloned.1.call-start
  6.5 1.5 copy.3
  8.0 0.7 constant_dynamic-slice_fusion.2
  8.8 0.0 all-gather.5.cloned.1.call-update
  8.8 0.0 all-gather.9.cloned.1.call-start
  8.8 1.7 constant_dynamic-slice_fusion.1
  10.5 0.0 all-gather.9.cloned.1.call-update
  10.5 0.0 all-gather.7.cloned.1.call-start
  10.6 80.1 %all-gather.5.cloned.1.call-done = bf16[512,2048]{0,1:T(8,128)(2,1)} async-done(((bf16[512,256]{0,1:T(8,128)(2,1)}), bf16[512,2048]{0,1:T(8,128)(2,1)}) %all-gather.5.cloned.1.call-update) | async-done | bytes 2097168 | tf_op jit(solution)/shard_map/all_gather | solution.py:21
  90.7 50.5 %all-gather.9.cloned.1.call-done = bf16[1,2048,1024]{2,1,0:T(8,128)(2,1)} async-done(((bf16[1,128,1024]{2,1,0:T(8,128)(2,1)}), bf16[1,2048,1024]{2,1,0:T(8,128)(2,1)}) %all-gather.9.cloned.1.call-update) | async-done | bytes 4194320 | tf_op jit(solution)/shard_map/all_gather | solution.py:26
  141.2 5.2 %fusion.2 = f32[512,1024]{1,0:T(8,128)S(1)} fusion(bf16[512,2048]{0,1:T(8,128)(2,1)} %all-gather.5.cloned.1.call-done, bf16[1,2048,1024]{2,1,0:T(8,128)(2,1)} %all-gather.9.cloned.1.call-done), kind=kOutput, calls=%fused_computation.2 | convolution fusion | flops 2147483648 | bytes 8388608 | tf_op jit(solution)/shard_map/dot_general | solution.py:24
  146.3 75.0 %all-reduce.1 = bf16[512,1024]{1,0:T(8,128)(2,1)S(1)} all-reduce(f32[512,1024]{1,0:T(8,128)S(1)} %fusion.2), channel_id=1, replica_groups=mesh['row'=16,'col'=8,'depth'=4] {'depth'}, use_global_device_ids=true, to_apply=%region_0.1 | all-reduce | flops 524288 | bytes 3145728 | tf_op jit(solution)/shard_map/psum | solution.py:31
  221.4 0.8 reshape.20
  222.1 0.5 constant_dynamic-slice_fusion
  222.7 1.3 copy.5
  224.0 0.0 all-gather.7.cloned.1.call-update
  224.0 0.0 reduce-scatter.2.cloned.1.call-start
  224.1 73.0 %all-gather.7.cloned.1.call-done = bf16[512,2048]{0,1:T(8,128)(2,1)} async-done(((bf16[512,256]{0,1:T(8,128)(2,1)}), bf16[512,2048]{0,1:T(8,128)(2,1)}) %all-gather.7.cloned.1.call-update) | async-done | bytes 2097168 | tf_op jit(solution)/shard_map/all_gather | solution.py:21
  297.1 6.5 %fusion.4 = f32[512,1024]{1,0:T(8,128)} fusion(bf16[512,2048]{0,1:T(8,128)(2,1)} %all-gather.7.cloned.1.call-done, bf16[1,2048,1024]{2,1,0:T(8,128)(2,1)} %all-gather.9.cloned.1.call-done), kind=kOutput, calls=%fused_computation.4 | convolution fusion | flops 2148007936 | bytes 8388608 | tf_op jit(solution)/shard_map/dot_general | solution.py:24
  303.6 0.0 reduce-scatter.2.cloned.1.call-update
  303.6 54.2 %reduce-scatter.2.cloned.1.call-done = f32[512,256]{1,0:T(8,128)} async-done(((f32[512,1024]{1,0:T(8,128)}), f32[512,256]{1,0:T(8,128)}) %reduce-scatter.2.cloned.1.call-update) | async-done | bytes 524304 | tf_op jit(solution)/shard_map/reduce_scatter | solution.py:36
  357.8 1.9 multiply_add_fusion
Async XLA Ops:
  6.5 84.1 %all-gather.5.cloned.1.call-start = ((), (), s32[]{:S(2)}) async-start(), calls=%async_computation.1 | async-start | bytes 2359296 | tf_op jit(solution)/shard_map/all_gather | solution.py:21
  8.8 132.4 %all-gather.9.cloned.1.call-start = ((), (), s32[]{:S(2)}) async-start(), calls=%async_computation.4 | async-start | bytes 4456448 | tf_op jit(solution)/shard_map/all_gather | solution.py:26
  10.5 286.6 %all-gather.7.cloned.1.call-start = ((), (), s32[]{:S(2)}) async-start(), calls=%async_computation.2 | async-start | bytes 2359296 | tf_op jit(solution)/shard_map/all_gather | solution.py:21
  224.0 133.8 %reduce-scatter.2.cloned.1.call-start = ((), (), s32[]{:S(2)}) async-start(), calls=%async_computation.3 | async-start | bytes 2621440 | tf_op jit(solution)/shard_map/reduce_scatter | solution.py:36
Sparse Core Ops, SparseCore 0:
  10.5 80.0 all-gather.4
  92.8 48.3 all-gather.8
  224.2 72.9 all-gather.6
  303.7 54.0 reduce-scatter.1
where the time goes:
time: 366 us
  waiting for transfers between devices  258 us (70%)
  blocking collectives  75 us (20%)
  between operations  13.2 us (4%)
  matrix products  11.6 us (3%)
  local copies, waits for them, and re-layouts  6.51 us (2%)
    all_gather x2, waiting for transfers between devices, gather_slab(): return lax.all_gather(local_slab, 'col', axis=1, tiled=True)  153 us
    psum x1, blocking collectives, on_device(): square = lax.psum(partial_square, 'depth').astype(jnp.bfloat16)  75 us
    reduce_scatter x1, waiting for transfers between devices, on_device(): lax.psum_scatter(-2.0 * partial_cube, 'depth', scatter_dimension=1, tiled...  54.2 us
    all_gather x1, waiting for transfers between devices, multiply(): lax.all_gather(row_strips, 'row', axis=0, tiled=True)  50.5 us
    dot_general x2, matrix products, multiply(): jnp.dot(left_full, lax.all_gather(row_strips, 'row', axis=0, tiled=True),...  11.6 us
  transfers between devices with their start and end apart: 4, of which 4 were waited for; matrix products, arithmetic and copies ran while one was open for 0% of the time, Pallas kernels for 0%

commit v1 on v0

v1 whole, which is shorter than its diff:
```python
import functools

import jax
import jax.numpy as jnp
from jax import lax
from jax.experimental import pallas as pl
from jax.experimental.pallas import tpu as pltpu
from jax.sharding import PartitionSpec as P

MESH = pl.DeviceIdType.MESH
F32 = jnp.float32
BF16 = jnp.bfloat16

CHUNKS = 4
STREAM = 4
SUB = 2
NT = (((1,), (1,)), ((), ()))


def rem(a, b):
    return lax.rem(a, jnp.int32(b))


def div(a, b):
    return lax.div(a, jnp.int32(b))


class Copies:
    def __init__(self):
        self.sent = []

    def start(self, src, dst, send, recv, device, when=None):
        copy = pltpu.make_async_remote_copy(
            src_ref=src, dst_ref=dst, send_sem=send, recv_sem=recv, device_id=device, device_id_type=MESH
        )
        if when is None:
            copy.start()
        else:
            pl.when(when)(copy.start)
        self.sent.append((when, copy.wait_send))

    def finish(self):
        for when, wait in self.sent:
            if when is None:
                wait()
            else:
                pl.when(when)(wait)


def kernel(
    a_ref, out_ref, other, bt, sb, part, relay, raw, summed,
    y_send, y_recv, z_inject, z_forward, z_recv, cross_send, cross_recv, own_send, own_recv, own_local,
    rs_send, rs_recv, ag_send, ag_recv,
):
    rows = a_ref.shape[0]
    width = a_ref.shape[1]
    share = width // 4
    row, col, yl = lax.axis_index("row"), lax.axis_index("col"), lax.axis_index("depth")
    z, core = div(row, 2), rem(row, 2)
    yh, x = div(col, 4), rem(col, 4)
    y = yh * 4 + yl

    def at_z(step, to_core):
        return (rem(z + 8 + step, 8) * 2 + to_core, col, yl)

    def at_y(step):
        to = rem(y + 8 + step, 8)
        return (row, div(to, 4) * 4 + x, rem(to, 4))

    def at_x(step):
        return (row, yh * 4 + rem(x + 4 + step, 4), yl)

    sibling = (z * 2 + 1 - core, col, yl)

    barrier = pltpu.get_barrier_semaphore()
    peers = [at_z(1, 0), at_z(1, 1), at_z(-1, 0), at_z(-1, 1), at_y(1), at_y(-1), at_x(1), at_x(-1), sibling]
    for peer in peers:
        pl.semaphore_signal(barrier, inc=1, device_id=peer, device_id_type=MESH)
    pl.semaphore_wait(barrier, len(peers))

    copies = Copies()

    def wait_recv(dst, sem):
        pltpu.make_async_remote_copy(
            src_ref=dst, dst_ref=dst, send_sem=sem, recv_sem=sem, device_id=sibling, device_id_type=MESH
        ).wait_recv()

    half = rows // 2
    q = rem(z + 8 - 4 * yh, 8)
    source_chip = q < 4
    non_source = q >= 4
    is_source = jnp.logical_and(source_chip, core == div(yl, 2))
    is_sibling = jnp.logical_and(source_chip, core != div(yl, 2))
    parity = rem(yl, 2)
    own_piece = rem(q, 4)
    qq = q + core * (rem(11 - q, 8) - q)
    late = div(rem(qq + 7, 8), 4)
    after_own = 1 - div(qq, 4)
    quarter = half // 2
    sub = quarter // SUB

    def ring_piece(t, of_core, place, is_late):
        piece = (1 - is_late) * rem(place + 7 - t, 4) + is_late * (3 - t)
        return piece + of_core * (3 - 2 * piece)

    def stream_rows(d, j):
        return pl.ds(d * half + (j % 2) * quarter + (j // 2) * (half // STREAM), half // STREAM)

    def inject(h, j):
        d, k = j % 2, j // 2
        offset = d * quarter + k * sub
        src_rows = pl.ds(pl.multiple_of(parity * half + offset, sub), sub)
        src = (a_ref if h == 0 else other).at[src_rows, :]
        dst = bt.at[own_piece, pl.ds(offset, sub), pl.ds(h * width, width)]
        n = h * 4 + j
        to = at_z(1, 0) if d == 0 else at_z(-1, 1)
        copies.start(src, dst, z_inject.at[n], z_recv.at[h * 8 + k], to, is_source)
        copies.start(src, dst, own_send.at[n], own_recv.at[n], sibling, is_source)
        pl.when(is_source)(pltpu.make_async_copy(src, dst, own_local.at[n]).start)

    def stream(d, j):
        at = stream_rows(d, j)
        n = d * STREAM + j
        wait_recv(other.at[at, :], y_recv.at[n])
        last = 3 if d == 0 else 0
        copies.start(
            other.at[at, :], other.at[at, :], y_send.at[8 + n], y_recv.at[n], at_y(1 if d == 0 else -1), yl != last
        )

    def ring(h, t, k):
        n = h * 8 + t * SUB + k
        piece = ring_piece(t, core, qq, late)
        at = bt.at[
            piece, pl.ds(pl.multiple_of(core * quarter + k * sub, sub), sub), pl.ds(h * width, width)
        ]
        if t == 3:
            pl.when(non_source)(lambda: wait_recv(at, z_recv.at[n]))
        else:
            wait_recv(at, z_recv.at[n])
        copies.start(at, at, cross_send.at[n], cross_recv.at[n], sibling, non_source if t == 3 else None)
        forward = {2: qq >= 3, 3: jnp.logical_and(qq >= 4, qq <= 6)}.get(t)
        to = (rem(z + 8 + 1 - 2 * core, 8) * 2 + core, col, yl)
        slot = h * 8 + (t + after_own) * SUB + k
        copies.start(at, at, z_forward.at[n], z_recv.at[slot], to, forward)

    for j in range(STREAM):
        inject(0, j)
        for d in range(2):
            at = stream_rows(d, j)
            first = 3 if d == 0 else 0
            n = d * STREAM + j
            copies.start(
                a_ref.at[at, :], other.at[at, :], y_send.at[n], y_recv.at[n], at_y(1 if d == 0 else -1), yl == first
            )
    for j in range(STREAM):
        for m in (2 * j, 2 * j + 1):
            ring(0, m // SUB, m % SUB)
        stream(0, j)
        stream(1, j)
        inject(1, j)
    for m in range(4 * SUB):
        ring(1, m // SUB, m % SUB)
    sib = 1 - core
    sib_qq = q + sib * (rem(11 - q, 8) - q)
    sib_late = div(rem(sib_qq + 7, 8), 4)
    for h in range(2):
        for t in range(4):
            for k in range(SUB):
                n = h * 8 + t * SUB + k
                piece = ring_piece(t, sib, sib_qq, sib_late)
                at = bt.at[
                    piece, pl.ds(pl.multiple_of(sib * quarter + k * sub, sub), sub), pl.ds(h * width, width)
                ]
                if t == 3:
                    pl.when(non_source)(functools.partial(wait_recv, at, cross_recv.at[n]))
                else:
                    wait_recv(at, cross_recv.at[n])
        for j in range(4):
            offset = (j % 2) * quarter + (j // 2) * sub
            at = bt.at[own_piece, pl.ds(offset, sub), pl.ds(h * width, width)]
            n = h * 4 + j
            pl.when(is_sibling)(functools.partial(wait_recv, at, own_recv.at[n]))
            pl.when(is_source)(
                pltpu.make_async_copy(
                    (a_ref if h == 0 else other).at[
                        pl.ds(pl.multiple_of(parity * half + offset, sub), sub), :
                    ],
                    at,
                    own_local.at[n],
                ).wait
            )

    chunk = rows // CHUNKS
    mid = chunk // 2
    ahead, behind, across = rem(x + 1, 4), rem(x + 3, 4), rem(x + 2, 4)

    def chunk_rows(i, which=None):
        if which is None:
            return pl.ds(i * chunk, chunk)
        return pl.ds(i * chunk + which * mid, mid)

    def multiply(r, i):
        at = chunk_rows(i)
        if r == 0:
            left = jnp.concatenate([a_ref[at, :], other[at, :]], axis=1)
        else:
            left = jnp.concatenate([sb[s, at, :] for s in range(8)], axis=1)

        @pl.loop(0, 4)
        def _(p):
            part[r, p, at, :] = lax.dot_general(left, bt[p], NT, preferred_element_type=F32)

    def rs(r, kind, d, i):
        n = ((r * 3 + kind) * 2 + d) * CHUNKS + i
        return rs_send.at[n], rs_recv.at[n]

    def spread(r, i):
        for d in range(2):
            to = at_x(1 - 2 * d)
            copies.start(part.at[r, across, chunk_rows(i, d), :], relay.at[r, d, i], *rs(r, 0, d, i), to)
        for d in range(2):
            to = at_x(1 - 2 * d)
            piece = ahead if d == 0 else behind
            copies.start(part.at[r, piece, chunk_rows(i, 1 - d), :], raw.at[r, d, i], *rs(r, 1, d, i), to)

    def pass_on(r, i):
        for d in range(2):
            to = at_x(1 - 2 * d)
            piece = ahead if d == 0 else behind
            at = chunk_rows(i, d)
            wait_recv(relay.at[r, d, i], rs(r, 0, d, i)[1])
            part[r, piece, at, :] = part[r, piece, at, :] + relay[r, d, i]
            copies.start(part.at[r, piece, at, :], summed.at[r, d, i], *rs(r, 2, d, i), to)

    def collect(r, i):
        for d in range(2):
            at = chunk_rows(i, d)
            wait_recv(raw.at[r, 1 - d, i], rs(r, 1, 1 - d, i)[1])
            wait_recv(summed.at[r, d, i], rs(r, 2, d, i)[1])
            total = part[r, x, at, :] + raw[r, 1 - d, i] + summed[r, d, i]
            if r == 0:
                sb[yl, at, :] = total.astype(BF16)
            else:
                out_ref[at, :] = 3.0 * sb[yl, at, :].astype(F32) - 2.0 * total

    def slot_of(y_from, y_at):
        return rem(div(y_from, 4) + div(y_at, 4), 2) * 4 + rem(y_from, 4)

    def gather(i, s):
        for d in range(2):
            sign = 1 - 2 * d
            y_from = rem(y + 8 - sign * s, 8)
            at = chunk_rows(i, d if s == 4 else None)
            here = sb.at[slot_of(y_from, y), at, :]
            if s > 0:
                wait_recv(here, ag_recv.at[(d * 5 + s) * CHUNKS + i])
            if s < 4:
                at = chunk_rows(i, d if s == 3 else None)
                y_to = rem(y + 8 + sign, 8)
                copies.start(
                    sb.at[slot_of(y_from, y), at, :],
                    sb.at[slot_of(y_from, y_to), at, :],
                    ag_send.at[(d * 5 + s) * CHUNKS + i],
                    ag_recv.at[(d * 5 + s + 1) * CHUNKS + i],
                    at_y(sign),
                )

    period = 4.8
    events = []
    for i in range(CHUNKS):
        t = i * period
        events += [
            (t, lambda i=i: (multiply(0, i), spread(0, i))),
            (t + 2.7, lambda i=i: pass_on(0, i)),
            (t + 6.6, lambda i=i: (collect(0, i), gather(i, 0))),
            (t + 9.1, lambda i=i: gather(i, 1)),
            (t + 11.6, lambda i=i: gather(i, 2)),
            (t + 14.1, lambda i=i: gather(i, 3)),
            (t + 16.1, lambda i=i: (gather(i, 4), multiply(1, i), spread(1, i))),
            (t + 18.8, lambda i=i: pass_on(1, i)),
            (t + 22.7, lambda i=i: collect(1, i)),
        ]
    for _, event in sorted(events, key=lambda e: e[0]):
        event()
    copies.finish()


def on_device(density):
    rows, width = density.shape
    share = width // 4
    chunk = rows // CHUNKS
    dma = pltpu.SemaphoreType.DMA
    return pl.pallas_call(
        kernel,
        out_shape=jax.ShapeDtypeStruct((rows, share), F32),
        in_specs=[pl.BlockSpec(memory_space=pltpu.VMEM)],
        out_specs=pl.BlockSpec(memory_space=pltpu.VMEM),
        scratch_shapes=[
            pltpu.VMEM((rows, width), BF16),
            pltpu.VMEM((4, share, 2 * width), BF16),
            pltpu.VMEM((8, rows, share), BF16),
            pltpu.VMEM((2, 4, rows, share), F32),
            pltpu.VMEM((2, 2, CHUNKS, chunk // 2, share), F32),
            pltpu.VMEM((2, 2, CHUNKS, chunk // 2, share), F32),
            pltpu.VMEM((2, 2, CHUNKS, chunk // 2, share), F32),
            dma((16,)),
            dma((8,)),
            dma((8,)),
            dma((16,)),
            dma((16,)),
            dma((16,)),
            dma((16,)),
            dma((8,)),
            dma((8,)),
            dma((8,)),
            dma((12 * CHUNKS,)),
            dma((12 * CHUNKS,)),
            dma((10 * CHUNKS,)),
            dma((10 * CHUNKS,)),
        ],
        compiler_params=pltpu.CompilerParams(
            collective_id=0, has_side_effects=True, vmem_limit_bytes=48 * 1024 * 1024
        ),
    )(density)


def solution(mesh):
    return jax.shard_map(
        on_device, mesh=mesh, in_specs=(P("row", "col"),), out_specs=P("row", ("col", "depth")), check_vma=False
    )
```

time: 366 us -> 228 us (0.62)
  the two profiles are of different devices: /device:TPU:1 before, /device:TPU:2 now
where the time goes in v1:
time: 228 us
  Pallas kernels  226 us (99%)
    pallas_call x1, Pallas kernels, on_device(): pl.pallas_call(kernel, out_shape=jax.ShapeDtypeStruct((rows, share), F32)...  226 us

profile of v1, /device:TPU:2, one launch (start us, length us, event | category | flops | bytes accessed | tf_op | source)
XLA Modules:
  0.0 227.8 jit_solution(16180791850342002888)
XLA Ops:
  0.0 0.0 copy-start
  0.0 1.2 copy-done
  1.2 225.8 %shard_map.17 = f32[512,256]{1,0:T(8,128)S(1)} custom-call(bf16[512,1024]{1,0:T(8,128)(2,1)S(1)} %copy-done), custom_call_target="tpu_custom_call" | custom-call | tf_op jit(solution)/shard_map/pallas_call | solution.py:293
  227.0 0.8 copy.3
Async XLA Ops:
  0.0 1.2 copy-start

commit v2 on v1

--- a/solution.py
+++ b/solution.py
@@ -12,9 +12,9 @@
 BF16 = jnp.bfloat16
 
 CHUNKS = 4
-STREAM = 4
-SUB = 2
-NT = (((1,), (1,)), ((), ()))
+STREAM = 8
+HOP = 2
+TICKS = 16 + 4 * HOP
 
 
 def rem(a, b):
@@ -23,6 +23,10 @@
 
 def div(a, b):
     return lax.div(a, jnp.int32(b))
+
+
+def rel_half(z, yh):
+    return rem(div(z, 4) + yh, 2)
 
 
 class Copies:
@@ -49,7 +53,7 @@
 
 def kernel(
     a_ref, out_ref, other, bt, sb, part, relay, raw, summed,
-    y_send, y_recv, z_inject, z_forward, z_recv, cross_send, cross_recv, own_send, own_recv, own_local,
+    x_send, x_recv, y_send, y_recv, z_inject, z_forward, z_recv, cross_send, cross_recv, own_send, own_recv, own_local,
     rs_send, rs_recv, ag_send, ag_recv,
 ):
     rows = a_ref.shape[0]
@@ -73,122 +77,187 @@
     sibling = (z * 2 + 1 - core, col, yl)
 
     barrier = pltpu.get_barrier_semaphore()
-    peers = [at_z(1, 0), at_z(1, 1), at_z(-1, 0), at_z(-1, 1), at_y(1), at_y(-1), at_x(1), at_x(-1), sibling]
+    peers = [at_z(1, 0), at_z(1, 1), at_z(-1, 0), at_z(-1, 1), at_y(1), at_y(-1), at_x(1), at_x(-1), at_x(2), sibling]
     for peer in peers:
         pl.semaphore_signal(barrier, inc=1, device_id=peer, device_id_type=MESH)
     pl.semaphore_wait(barrier, len(peers))
 
     copies = Copies()
 
+    def remote(src, dst, send, recv, device):
+        return pltpu.make_async_remote_copy(
+            src_ref=src, dst_ref=dst, send_sem=send, recv_sem=recv, device_id=device, device_id_type=MESH
+        )
+
+    def start(src, dst, send, recv, device):
+        remote(src, dst, send, recv, device).start()
+
     def wait_recv(dst, sem):
-        pltpu.make_async_remote_copy(
-            src_ref=dst, dst_ref=dst, send_sem=sem, recv_sem=sem, device_id=sibling, device_id_type=MESH
-        ).wait_recv()
+        remote(dst, dst, sem, sem, sibling).wait_recv()
+
+    def wait_send(src, sem):
+        remote(src, src, sem, sem, sibling).wait_send()
 
     half = rows // 2
-    q = rem(z + 8 - 4 * yh, 8)
-    source_chip = q < 4
-    non_source = q >= 4
-    is_source = jnp.logical_and(source_chip, core == div(yl, 2))
-    is_sibling = jnp.logical_and(source_chip, core != div(yl, 2))
-    parity = rem(yl, 2)
-    own_piece = rem(q, 4)
-    qq = q + core * (rem(11 - q, 8) - q)
-    late = div(rem(qq + 7, 8), 4)
-    after_own = 1 - div(qq, 4)
-    quarter = half // 2
-    sub = quarter // SUB
-
-    def ring_piece(t, of_core, place, is_late):
-        piece = (1 - is_late) * rem(place + 7 - t, 4) + is_late * (3 - t)
-        return piece + of_core * (3 - 2 * piece)
-
-    def stream_rows(d, j):
-        return pl.ds(d * half + (j % 2) * quarter + (j // 2) * (half // STREAM), half // STREAM)
-
-    def inject(h, j):
-        d, k = j % 2, j // 2
-        offset = d * quarter + k * sub
-        src_rows = pl.ds(pl.multiple_of(parity * half + offset, sub), sub)
-        src = (a_ref if h == 0 else other).at[src_rows, :]
-        dst = bt.at[own_piece, pl.ds(offset, sub), pl.ds(h * width, width)]
-        n = h * 4 + j
-        to = at_z(1, 0) if d == 0 else at_z(-1, 1)
-        copies.start(src, dst, z_inject.at[n], z_recv.at[h * 8 + k], to, is_source)
-        copies.start(src, dst, own_send.at[n], own_recv.at[n], sibling, is_source)
-        pl.when(is_source)(pltpu.make_async_copy(src, dst, own_local.at[n]).start)
+    strip = half // STREAM
+    block = half
+    up = rem(z + 8 - x, 4)
+    w = up + core * (rem(4 - up, 4) - up)
+    is_source = w == 0
+    away = w + 4 * (1 - lax.min(w, jnp.int32(1)))
+    passed = rel_half(rem(z + 8 - (1 - 2 * core) * away, 8), yh)
+    held = rel_half(z, yh)
+    next_z = at_z(1 - 2 * core, core)
+
+    def gray(e):
+        return e + div(e, 2) * (5 - 2 * e)
+
+    def tile(which, e, c, k):
+        at = pl.ds(pl.multiple_of(c * rows + k * block, block), block)
+        return bt.at[which, rem(x + gray(e), 4), at, :]
+
+    own_cols = pl.ds(pl.multiple_of(yl * share, share), share)
+
+    def inject(i, e, k, src):
+        dst = tile(held, e, core, k)
+        m = i * 2 + core
+        start(src, dst, z_inject.at[i], z_recv.at[m], at_z(1, 0))
+        start(src, dst, z_inject.at[8 + i], z_recv.at[m], at_z(-1, 1))
+        start(src, dst, own_send.at[i], own_recv.at[i], sibling)
+
+    def ring_chunk(m):
+        i, c = div(m, 2), rem(m, 2)
+        return tile(passed, div(i, 2), c, rem(i, 2)), c
+
+    def passes(c):
+        return jnp.logical_or(w < 3, c == core)
+
+    def ring(m):
+        at, c = ring_chunk(m)
+
+        @pl.when(jnp.logical_or(w > 0, c == core))
+        def _():
+            wait_recv(at, z_recv.at[m])
+            start(at, at, cross_send.at[m], cross_recv.at[m], sibling)
+
+            @pl.when(jnp.logical_and(w > 0, passes(c)))
+            def _():
+                start(at, at, z_forward.at[m], z_recv.at[m], next_z)
+
+    def strip_rows(d, j):
+        return pl.ds(pl.multiple_of(d * half + j * strip, strip), strip)
 
     def stream(d, j):
-        at = stream_rows(d, j)
+        at = strip_rows(d, j)
         n = d * STREAM + j
         wait_recv(other.at[at, :], y_recv.at[n])
-        last = 3 if d == 0 else 0
-        copies.start(
-            other.at[at, :], other.at[at, :], y_send.at[8 + n], y_recv.at[n], at_y(1 if d == 0 else -1), yl != last
-        )
-
-    def ring(h, t, k):
-        n = h * 8 + t * SUB + k
-        piece = ring_piece(t, core, qq, late)
-        at = bt.at[
-            piece, pl.ds(pl.multiple_of(core * quarter + k * sub, sub), sub), pl.ds(h * width, width)
-        ]
-        if t == 3:
-            pl.when(non_source)(lambda: wait_recv(at, z_recv.at[n]))
-        else:
-            wait_recv(at, z_recv.at[n])
-        copies.start(at, at, cross_send.at[n], cross_recv.at[n], sibling, non_source if t == 3 else None)
-        forward = {2: qq >= 3, 3: jnp.logical_and(qq >= 4, qq <= 6)}.get(t)
-        to = (rem(z + 8 + 1 - 2 * core, 8) * 2 + core, col, yl)
-        slot = h * 8 + (t + after_own) * SUB + k
-        copies.start(at, at, z_forward.at[n], z_recv.at[slot], to, forward)
-
-    for j in range(STREAM):
-        inject(0, j)
-        for d in range(2):
-            at = stream_rows(d, j)
-            first = 3 if d == 0 else 0
-            n = d * STREAM + j
-            copies.start(
-                a_ref.at[at, :], other.at[at, :], y_send.at[n], y_recv.at[n], at_y(1 if d == 0 else -1), yl == first
-            )
-    for j in range(STREAM):
-        for m in (2 * j, 2 * j + 1):
-            ring(0, m // SUB, m % SUB)
-        stream(0, j)
-        stream(1, j)
-        inject(1, j)
-    for m in range(4 * SUB):
-        ring(1, m // SUB, m % SUB)
-    sib = 1 - core
-    sib_qq = q + sib * (rem(11 - q, 8) - q)
-    sib_late = div(rem(sib_qq + 7, 8), 4)
-    for h in range(2):
-        for t in range(4):
-            for k in range(SUB):
-                n = h * 8 + t * SUB + k
-                piece = ring_piece(t, sib, sib_qq, sib_late)
-                at = bt.at[
-                    piece, pl.ds(pl.multiple_of(sib * quarter + k * sub, sub), sub), pl.ds(h * width, width)
-                ]
-                if t == 3:
-                    pl.when(non_source)(functools.partial(wait_recv, at, cross_recv.at[n]))
-                else:
-                    wait_recv(at, cross_recv.at[n])
-        for j in range(4):
-            offset = (j % 2) * quarter + (j // 2) * sub
-            at = bt.at[own_piece, pl.ds(offset, sub), pl.ds(h * width, width)]
-            n = h * 4 + j
-            pl.when(is_sibling)(functools.partial(wait_recv, at, own_recv.at[n]))
-            pl.when(is_source)(
-                pltpu.make_async_copy(
-                    (a_ref if h == 0 else other).at[
-                        pl.ds(pl.multiple_of(parity * half + offset, sub), sub), :
-                    ],
-                    at,
-                    own_local.at[n],
-                ).wait
-            )
+
+        @pl.when(yl != 3 * (1 - d))
+        def _():
+            start(other.at[at, :], other.at[at, :], y_send.at[n], y_recv.at[n], at_y(1 - 2 * d))
+
+    for k in range(2):
+        src = a_ref.at[pl.ds(k * block, block), own_cols]
+
+        @pl.when(is_source)
+        def _():
+            inject(k, jnp.int32(0), jnp.int32(k), src)
+            pltpu.make_async_copy(src, tile(held, jnp.int32(0), core, jnp.int32(k)), own_local.at[k]).start()
+
+        @pl.when(w > 0)
+        def _():
+            to = rem(z, 4)
+            e = gray(rem(x + 4 - to, 4))
+            dst = bt.at[held, x, pl.ds(pl.multiple_of(core * rows + k * block, block), block), :]
+            start(src, dst, x_send.at[k], x_recv.at[e * 2 + k], (row, yh * 4 + to, yl))
+
+    for d in range(2):
+
+        @pl.when(yl == 3 * (1 - d))
+        def _():
+            for j in range(STREAM):
+                at = strip_rows(d, j)
+                n = d * STREAM + j
+                start(a_ref.at[at, :], other.at[at, :], y_send.at[n], y_recv.at[n], at_y(1 - 2 * d))
+
+    @pl.loop(0, TICKS)
+    def _(tick):
+        i = div(tick, 2) + 1
+
+        @pl.when(is_source & (rem(tick, 2) == 0) & (i >= 2) & (i < 8))
+        def _():
+            e, k = div(i, 2), rem(i, 2)
+            src = tile(held, e, core, k)
+            wait_recv(src, x_recv.at[i])
+            inject(i, e, k, src)
+
+        m = tick - HOP * away
+
+        @pl.when((m >= 0) & (m < 16))
+        def _():
+            ring(m)
+
+        for d in range(2):
+            j = tick - HOP * (yl + 1 if d == 0 else 4 - yl)
+
+            @pl.when((j >= 0) & (j < STREAM))
+            def _():
+                stream(d, j)
+
+    sib_w = rem(4 - w, 4)
+    sib_away = sib_w + 4 * (1 - lax.min(sib_w, jnp.int32(1)))
+    sib_passed = rel_half(rem(z + 8 + (1 - 2 * core) * sib_away, 8), yh)
+
+    @pl.loop(0, 16)
+    def _(m):
+        i, c = div(m, 2), rem(m, 2)
+
+        @pl.when(jnp.logical_or(w > 0, c != core))
+        def _():
+            wait_recv(tile(sib_passed, div(i, 2), c, rem(i, 2)), cross_recv.at[m])
+
+    @pl.when(is_source)
+    def _():
+        for k in range(2):
+            src = a_ref.at[pl.ds(k * block, block), own_cols]
+            pltpu.make_async_copy(src, tile(held, jnp.int32(0), core, jnp.int32(k)), own_local.at[k]).wait()
+
+        @pl.loop(0, 8)
+        def _(i):
+            wait_recv(tile(held, div(i, 2), 1 - core, rem(i, 2)), own_recv.at[i])
+
+    def finish_operands():
+        for k in range(2):
+
+            @pl.when(w > 0)
+            def _():
+                wait_send(bt.at[held, x, pl.ds(0, block), :], x_send.at[k])
+
+        @pl.when(is_source)
+        def _():
+            @pl.loop(0, 8)
+            def _(i):
+                src = tile(held, div(i, 2), core, rem(i, 2))
+                wait_send(src, z_inject.at[i])
+                wait_send(src, z_inject.at[8 + i])
+                wait_send(src, own_send.at[i])
+
+        @pl.loop(0, 16)
+        def _(m):
+            at, c = ring_chunk(m)
+
+            @pl.when(jnp.logical_or(w > 0, c == core))
+            def _():
+                wait_send(at, cross_send.at[m])
+
+                @pl.when(jnp.logical_and(w > 0, passes(c)))
+                def _():
+                    wait_send(at, z_forward.at[m])
+
+        @pl.loop(0, 2 * STREAM)
+        def _(n):
+            at = pl.ds(pl.multiple_of(n * strip, strip), strip)
+            wait_send(other.at[at, :], y_send.at[n])
 
     chunk = rows // CHUNKS
     mid = chunk // 2
@@ -208,7 +277,8 @@
 
         @pl.loop(0, 4)
         def _(p):
-            part[r, p, at, :] = lax.dot_general(left, bt[p], NT, preferred_element_type=F32)
+            right = jnp.concatenate([bt[0, p], bt[1, p]], axis=0)
+            part[r, p, at, :] = jnp.dot(left, right, preferred_element_type=F32)
 
     def rs(r, kind, d, i):
         n = ((r * 3 + kind) * 2 + d) * CHUNKS + i
@@ -283,6 +353,7 @@
     for _, event in sorted(events, key=lambda e: e[0]):
         event()
     copies.finish()
+    finish_operands()
 
 
 def on_device(density):
@@ -297,22 +368,24 @@
         out_specs=pl.BlockSpec(memory_space=pltpu.VMEM),
         scratch_shapes=[
             pltpu.VMEM((rows, width), BF16),
-            pltpu.VMEM((4, share, 2 * width), BF16),
+            pltpu.VMEM((2, 4, 2 * rows, share), BF16),
             pltpu.VMEM((8, rows, share), BF16),
             pltpu.VMEM((2, 4, rows, share), F32),
             pltpu.VMEM((2, 2, CHUNKS, chunk // 2, share), F32),
             pltpu.VMEM((2, 2, CHUNKS, chunk // 2, share), F32),
             pltpu.VMEM((2, 2, CHUNKS, chunk // 2, share), F32),
+            dma((2,)),
+            dma((8,)),
+            dma((2 * STREAM,)),
+            dma((2 * STREAM,)),
             dma((16,)),
-            dma((8,)),
-            dma((8,)),
             dma((16,)),
             dma((16,)),
             dma((16,)),
             dma((16,)),
             dma((8,)),
             dma((8,)),
-            dma((8,)),
+            dma((2,)),
             dma((12 * CHUNKS,)),
             dma((12 * CHUNKS,)),
             dma((10 * CHUNKS,)),

time: 228 us -> 119 us (0.52)
  the two profiles are of different devices: /device:TPU:2 before, /device:TPU:66 now
where the time goes in v2:
time: 119 us
  Pallas kernels  117 us (98%)
  local copies, waits for them, and re-layouts  2.02 us (2%)
    pallas_call x1, Pallas kernels, on_device(): pl.pallas_call(kernel, out_shape=jax.ShapeDtypeStruct((rows, share), F32)...  117 us

profile of v2, /device:TPU:66, one launch (start us, length us, event | category | flops | bytes accessed | tf_op | source)
XLA Modules:
  0.0 119.2 jit_solution(5670494470606430353)
XLA Ops:
  0.0 0.0 copy-start
  0.0 1.2 %copy-done = bf16[512,1024]{1,0:T(8,128)(2,1)S(1)} copy-done((bf16[512,1024]{1,0:T(8,128)(2,1)S(1)}, bf16[512,1024]{1,0:T(8,128)(2,1)}, u32[]{:S(2)}) %copy-start) | copy-done | bytes 1048600
  1.2 117.1 %shard_map.17 = f32[512,256]{1,0:T(8,128)S(1)} custom-call(bf16[512,1024]{1,0:T(8,128)(2,1)S(1)} %copy-done), custom_call_target="tpu_custom_call" | custom-call | tf_op jit(solution)/shard_map/pallas_call | solution.py:364
  118.4 0.8 copy.3
Async XLA Ops:
  0.0 1.2 %copy-start = (bf16[512,1024]{1,0:T(8,128)(2,1)S(1)}, bf16[512,1024]{1,0:T(8,128)(2,1)}, u32[]{:S(2)}) copy-start(bf16[512,1024]{1,0:T(8,128)(2,1)} %a_ref.1) | copy-start | bytes 3145732

commit v3 on v0

v3 whole, which is shorter than its diff:
```python
import jax
import jax.numpy as jnp
from jax import lax
from jax.experimental import pallas as pl
from jax.experimental.pallas import tpu as pltpu
from jax.sharding import PartitionSpec as P

MESH = pl.DeviceIdType.MESH
F32 = jnp.float32
BF16 = jnp.bfloat16

GROUPS = 2
SQUARE = 4
CUBE = 4
SPLIT = 2
UNITS = 8 * SPLIT
STREAM = 8 * SPLIT
HOP = 5
TICK = 0.75
TICKS = 2 * UNITS + 4 * HOP
PASS, COLLECT, RING, PERIOD = 4.1, 7.8, 3.5, 2.4
PASS_CUBE, COLLECT_CUBE, PERIOD_CUBE = 5.5, 10.5, 4.5


def rem(a, b):
    return lax.rem(a, jnp.int32(b))


def div(a, b):
    return lax.div(a, jnp.int32(b))


def rel_half(z, yh):
    return rem(div(z, 4) + yh, 2)


def gray(e):
    return e + div(e, 2) * (5 - 2 * e)


def kernel(
    a_hbm, out_ref, a_ref, own, other, bt, sb, part1, part2, relay1, raw1, summed1, relay2, raw2, summed2,
    x_send, x_recv, y_send, y_recv, z_inject, z_forward, z_recv, cross_send, cross_recv, own_send, own_recv, own_local, load,
    rs1_send, rs1_recv, rs2_send, rs2_recv, ag_send, ag_recv,
):
    rows, width = a_hbm.shape
    share = width // 4
    cols = share // GROUPS
    row, col, yl = lax.axis_index("row"), lax.axis_index("col"), lax.axis_index("depth")
    z, core = div(row, 2), rem(row, 2)
    yh, x = div(col, 4), rem(col, 4)
    y = yh * 4 + yl

    def at_z(step, to_core):
        return (rem(z + 8 + step, 8) * 2 + to_core, col, yl)

    def at_y(step):
        to = rem(y + 8 + step, 8)
        return (row, div(to, 4) * 4 + x, rem(to, 4))

    def at_x(step):
        return (row, yh * 4 + rem(x + 4 + step, 4), yl)

    sibling = (z * 2 + 1 - core, col, yl)

    loads = [
        pltpu.make_async_copy(
            a_hbm.at[:, pl.ds(pl.multiple_of(yl * share + g * cols, cols), cols)], own.at[g], load.at[g]
        )
        for g in range(GROUPS)
    ] + [pltpu.make_async_copy(a_hbm, a_ref, load.at[GROUPS])]
    for copy in loads:
        copy.start()

    barrier = pltpu.get_barrier_semaphore()
    peers = [at_z(1, 0), at_z(1, 1), at_z(-1, 0), at_z(-1, 1), at_y(1), at_y(-1), at_x(1), at_x(-1), at_x(2), sibling]
    for peer in peers:
        pl.semaphore_signal(barrier, inc=1, device_id=peer, device_id_type=MESH)
    for copy in loads:
        copy.wait()
    pl.semaphore_wait(barrier, len(peers))

    def remote(src, dst, send, recv, device):
        return pltpu.make_async_remote_copy(
            src_ref=src, dst_ref=dst, send_sem=send, recv_sem=recv, device_id=device, device_id_type=MESH
        )

    def start(src, dst, send, recv, device):
        remote(src, dst, send, recv, device).start()

    def wait_recv(dst, sem):
        remote(dst, dst, sem, sem, sibling).wait_recv()

    def wait_send(src, sem):
        remote(src, src, sem, sem, sibling).wait_send()

    half = rows // 2
    strip = half // STREAM
    up = rem(z + 8 - x, 4)
    w = up + core * (rem(4 - up, 4) - up)
    is_source = w == 0
    away = w + 4 * (1 - lax.min(w, jnp.int32(1)))
    passed = rel_half(rem(z + 8 - (1 - 2 * core) * away, 8), yh)
    held = rel_half(z, yh)
    next_z = at_z(1 - 2 * core, core)

    unit = rows // SPLIT

    def tile(which, i, c):
        n, k = div(i, SPLIT), rem(i, SPLIT)
        u = div(n + 1, 3)
        others = lax.min(u, jnp.int32(1))
        g = others * (u - 1) + (1 - others) * n
        e = others * (rem(n + 1, 3) + 1)
        at = pl.ds(pl.multiple_of(c * rows + k * unit, unit), unit)
        return bt.at[which, g, rem(x + gray(e), 4), at, :]

    def own_piece(g, k):
        return own.at[g, pl.ds(k * unit, unit), :]

    def own_copy(g, k):
        i = g * SPLIT + k
        return pltpu.make_async_copy(own_piece(g, k), tile(held, jnp.int32(i), core), own_local.at[i])

    def inject(i, src):
        dst = tile(held, i, core)
        m = i * 2 + core
        start(src, dst, z_inject.at[i], z_recv.at[m], at_z(1, 0))
        start(src, dst, z_inject.at[UNITS + i], z_recv.at[m], at_z(-1, 1))
        start(src, dst, own_send.at[i], own_recv.at[i], sibling)

    def passes(c):
        return (w > 0) & ((w < 3) | (c == core))

    def ring(m):
        i, c = div(m, 2), rem(m, 2)
        at = tile(passed, i, c)

        @pl.when((w > 0) | (c == core))
        def _():
            wait_recv(at, z_recv.at[m])

            @pl.when(passes(c))
            def _():
                start(at, at, z_forward.at[m], z_recv.at[m], next_z)

            start(at, at, cross_send.at[m], cross_recv.at[m], sibling)

    def strip_rows(d, j):
        return pl.ds(pl.multiple_of(d * half + j * strip, strip), strip)

    def stream(d, j):
        at = strip_rows(d, j)
        n = d * STREAM + j
        wait_recv(other.at[at, :], y_recv.at[n])

        @pl.when(yl != 3 * (1 - d))
        def _():
            start(other.at[at, :], other.at[at, :], y_send.at[n], y_recv.at[n], at_y(1 - 2 * d))

    @pl.when(is_source)
    def _():
        for g in range(GROUPS):
            for k in range(SPLIT):
                inject(jnp.int32(g * SPLIT + k), own_piece(g, k))
        for g in range(GROUPS):
            for k in range(SPLIT):
                own_copy(g, k).start()

    @pl.when(w > 0)
    def _():
        to = rem(z, 4)
        e = gray(rem(x + 4 - to, 4))
        for g in range(GROUPS):
            for k in range(SPLIT):
                dst = bt.at[held, g, x, pl.ds(pl.multiple_of(core * rows + k * unit, unit), unit), :]
                arrival = x_recv.at[(e + 1 + 3 * g) * SPLIT + k]
                start(own_piece(g, k), dst, x_send.at[g * SPLIT + k], arrival, (row, yh * 4 + to, yl))

    for d in range(2):

        @pl.when(yl == 3 * (1 - d))
        def _():
            for j in range(STREAM):
                at = strip_rows(d, j)
                n = d * STREAM + j
                start(a_ref.at[at, :], other.at[at, :], y_send.at[n], y_recv.at[n], at_y(1 - 2 * d))

    def tick(t):
        i = t

        @pl.when(is_source & (i >= 2 * SPLIT) & (i < UNITS))
        def _():
            src = tile(held, i, core)
            wait_recv(src, x_recv.at[i])
            inject(i, src)

        m = t - HOP * away

        @pl.when((m >= 0) & (m < 2 * UNITS))
        def _():
            ring(m)

        for d in range(2):
            j = t - HOP * (yl + 1 if d == 0 else 4 - yl)

            @pl.when((j >= 0) & (j < STREAM))
            def _():
                stream(d, j)

    sib_w = rem(4 - w, 4)
    sib_away = sib_w + 4 * (1 - lax.min(sib_w, jnp.int32(1)))
    sib_passed = rel_half(rem(z + 8 + (1 - 2 * core) * sib_away, 8), yh)

    def arrived(g):
        first, after = (0, 5 * SPLIT) if g == 0 else (5 * SPLIT, UNITS)

        @pl.loop(2 * first, 2 * after)
        def _(m):
            i, c = div(m, 2), rem(m, 2)

            @pl.when((w > 0) | (c != core))
            def _():
                wait_recv(tile(sib_passed, i, c), cross_recv.at[m])

        @pl.when(is_source)
        def _():
            if g == 0:
                for i in range(2 * SPLIT):
                    own_copy(i // SPLIT, i % SPLIT).wait()

            @pl.loop(first, after)
            def _(i):
                wait_recv(tile(held, i, 1 - core), own_recv.at[i])

    def finish_operands():
        @pl.when(w > 0)
        def _():
            for i in range(2 * SPLIT):
                wait_send(bt.at[held, 0, x, pl.ds(0, unit), :], x_send.at[i])

        @pl.when(is_source)
        def _():
            @pl.loop(0, UNITS)
            def _(i):
                src = tile(held, i, core)
                wait_send(src, z_inject.at[i])
                wait_send(src, z_inject.at[UNITS + i])
                wait_send(src, own_send.at[i])

        @pl.loop(0, 2 * UNITS)
        def _(m):
            i, c = div(m, 2), rem(m, 2)
            at = tile(passed, i, c)

            @pl.when((w > 0) | (c == core))
            def _():
                wait_send(at, cross_send.at[m])

                @pl.when(passes(c))
                def _():
                    wait_send(at, z_forward.at[m])

        @pl.loop(0, 2 * STREAM)
        def _(n):
            at = pl.ds(pl.multiple_of(n * strip, strip), strip)
            wait_send(other.at[at, :], y_send.at[n])

    ahead, behind, across = rem(x + 1, 4), rem(x + 3, 4), rem(x + 2, 4)
    sent = []

    def send(src, dst, send_sem, recv_sem, device):
        copy = remote(src, dst, send_sem, recv_sem, device)
        copy.start()
        sent.append(copy.wait_send)

    class Sum:
        def __init__(self, part, relay, raw, summed, sends, recvs, chunk):
            self.part, self.relay, self.raw, self.summed = part, relay, raw, summed
            self.sends, self.recvs, self.mid = sends, recvs, chunk // 2
            self.slots = relay.shape[1]

        def at(self, piece, i, which):
            g, r = i
            rows_at = pl.ds((2 * r + which) * self.mid, self.mid)
            return (g, piece, rows_at, slice(None)) if g is not None else (piece, rows_at, slice(None))

        def slot(self, i):
            return i[0] * SQUARE + i[1] if i[0] is not None else i[1]

        def sems(self, kind, d, i):
            n = (kind * 2 + d) * self.slots + self.slot(i)
            return self.sends.at[n], self.recvs.at[n]

        def spread(self, i):
            n = self.slot(i)
            for d in range(2):
                src = self.part.at[self.at(across, i, d)]
                send(src, self.relay.at[d, n], *self.sems(0, d, i), at_x(1 - 2 * d))
            for d in range(2):
                src = self.part.at[self.at(ahead if d == 0 else behind, i, 1 - d)]
                send(src, self.raw.at[d, n], *self.sems(1, d, i), at_x(1 - 2 * d))

        def pass_on(self, i):
            n = self.slot(i)
            for d in range(2):
                wait_recv(self.relay.at[d, n], self.sems(0, d, i)[1])
                at = self.at(ahead if d == 0 else behind, i, d)
                self.part[at] = self.part[at] + self.relay[d, n]
                send(self.part.at[at], self.summed.at[d, n], *self.sems(2, d, i), at_x(1 - 2 * d))

        def collect(self, i):
            n = self.slot(i)
            totals = []
            for d in range(2):
                wait_recv(self.raw.at[1 - d, n], self.sems(1, 1 - d, i)[1])
                wait_recv(self.summed.at[d, n], self.sems(2, d, i)[1])
                totals.append(self.part[self.at(x, i, d)] + self.raw[1 - d, n] + self.summed[d, n])
            return totals

    square_chunk, cube_chunk = rows // SQUARE, rows // CUBE
    square_sum = Sum(part1, relay1, raw1, summed1, rs1_send, rs1_recv, square_chunk)
    cube_sum = Sum(part2, relay2, raw2, summed2, rs2_send, rs2_recv, cube_chunk)

    def multiply_square(g, r):
        at = pl.ds(r * square_chunk, square_chunk)
        left = jnp.concatenate([a_ref[at, :], other[at, :]], axis=1)

        @pl.loop(0, 4, step=2)
        def _(p):
            right = jnp.concatenate(
                [jnp.concatenate([bt[h, g, p], bt[h, g, p + 1]], axis=1) for h in range(2)], axis=0
            )
            product = jnp.dot(left, right, preferred_element_type=F32)
            part1[g, p, at, :] = product[:, :cols]
            part1[g, p + 1, at, :] = product[:, cols:]

    def round_square(g, r):
        mid = square_chunk // 2
        for d, total in enumerate(square_sum.collect((g, r))):
            sb[g, yl, pl.ds((2 * r + d) * mid, mid), :] = total.astype(BF16)

    def slot_of(y_from, y_at):
        return rem(div(y_from, 4) + div(y_at, 4), 2) * 4 + rem(y_from, 4)

    def gather(g, r, s):
        mid = square_chunk // 2
        slots = GROUPS * SQUARE
        n = g * SQUARE + r

        def part(d, last):
            return pl.ds((2 * r + d) * mid, mid) if last else pl.ds(r * square_chunk, square_chunk)

        for d in range(2):
            sign = 1 - 2 * d
            y_from = rem(y + 8 - sign * s, 8)
            if s > 0:
                here = sb.at[g, slot_of(y_from, y), part(d, s == 4), :]
                wait_recv(here, ag_recv.at[(d * 5 + s) * slots + n])
            if s < 4:
                at = part(d, s == 3)
                y_to = rem(y + 8 + sign, 8)
                send(
                    sb.at[g, slot_of(y_from, y), at, :],
                    sb.at[g, slot_of(y_from, y_to), at, :],
                    ag_send.at[(d * 5 + s) * slots + n],
                    ag_recv.at[(d * 5 + s + 1) * slots + n],
                    at_y(sign),
                )

    def multiply_cube(r):
        at = pl.ds(r * cube_chunk, cube_chunk)
        left = jnp.concatenate([sb[g, s, at, :] for s in range(8) for g in range(GROUPS)], axis=1)

        @pl.loop(0, 4)
        def _(p):
            right = jnp.concatenate(
                [jnp.concatenate([bt[h, g, p] for g in range(GROUPS)], axis=1) for h in range(2)], axis=0
            )
            part2[p, at, :] = jnp.dot(left, right, preferred_element_type=F32)

    def purify(r):
        mid = cube_chunk // 2
        for d, total in enumerate(cube_sum.collect((None, r))):
            at = pl.ds((2 * r + d) * mid, mid)
            own = jnp.concatenate([sb[g, yl, at, :] for g in range(GROUPS)], axis=1).astype(F32)
            out_ref[at, :] = 3.0 * own - 2.0 * total

    events = []
    last = {}
    for g in range(GROUPS):
        begin = TICK * (2 * SPLIT * (5 if g == 0 else 8) + 4 * HOP)
        for r in range(SQUARE):
            t = begin + r * PERIOD
            if r == 0:
                events.append((t, lambda g=g: arrived(g)))
            events += [
                (t, lambda g=g, r=r: (multiply_square(g, r), square_sum.spread((g, r)))),
                (t + PASS, lambda g=g, r=r: square_sum.pass_on((g, r))),
                (t + COLLECT, lambda g=g, r=r: (round_square(g, r), gather(g, r, 0))),
            ]
            for s in range(1, 5):
                events.append((t + COLLECT + RING * s, lambda g=g, r=r, s=s: gather(g, r, s)))
            last[r] = t + COLLECT + RING * 4
    t = 0.0
    for r in range(CUBE):
        t = max(t + PERIOD_CUBE, last[(r + 1) * SQUARE // CUBE - 1])
        events += [
            (t, lambda r=r: (multiply_cube(r), cube_sum.spread((None, r)))),
            (t + PASS_CUBE, lambda r=r: cube_sum.pass_on((None, r))),
            (t + COLLECT_CUBE, lambda r=r: purify(r)),
        ]
    done = 0
    for t, event in sorted(events, key=lambda e: e[0]):
        due = min(TICKS, int(t / TICK))
        if due > done:
            pl.loop(done, due)(tick)
            done = due
        event()
    for wait in sent:
        wait()
    finish_operands()


def on_device(density):
    rows, width = density.shape
    share = width // 4
    cols = share // GROUPS
    dma = pltpu.SemaphoreType.DMA
    square_parts = pltpu.VMEM((2, GROUPS * SQUARE, rows // SQUARE // 2, cols), F32)
    cube_parts = pltpu.VMEM((2, CUBE, rows // CUBE // 2, share), F32)
    return pl.pallas_call(
        kernel,
        out_shape=jax.ShapeDtypeStruct((rows, share), F32),
        in_specs=[pl.BlockSpec(memory_space=pl.ANY)],
        out_specs=pl.BlockSpec(memory_space=pltpu.VMEM),
        scratch_shapes=[
            pltpu.VMEM((rows, width), BF16),
            pltpu.VMEM((GROUPS, rows, cols), BF16),
            pltpu.VMEM((rows, width), BF16),
            pltpu.VMEM((2, GROUPS, 4, 2 * rows, cols), BF16),
            pltpu.VMEM((GROUPS, 8, rows, cols), BF16),
            pltpu.VMEM((GROUPS, 4, rows, cols), F32),
            pltpu.VMEM((4, rows, share), F32),
            square_parts,
            square_parts,
            square_parts,
            cube_parts,
            cube_parts,
            cube_parts,
            dma((2 * SPLIT,)),
            dma((UNITS,)),
            dma((2 * STREAM,)),
            dma((2 * STREAM,)),
            dma((2 * UNITS,)),
            dma((2 * UNITS,)),
            dma((2 * UNITS,)),
            dma((2 * UNITS,)),
            dma((2 * UNITS,)),
            dma((UNITS,)),
            dma((UNITS,)),
            dma((2 * SPLIT,)),
            dma((GROUPS + 1,)),
            dma((6 * GROUPS * SQUARE,)),
            dma((6 * GROUPS * SQUARE,)),
            dma((6 * CUBE,)),
            dma((6 * CUBE,)),
            dma((10 * GROUPS * SQUARE,)),
            dma((10 * GROUPS * SQUARE,)),
        ],
        compiler_params=pltpu.CompilerParams(
            collective_id=0, has_side_effects=True, vmem_limit_bytes=48 * 1024 * 1024
        ),
    )(density)


def solution(mesh):
    return jax.shard_map(
        on_device, mesh=mesh, in_specs=(P("row", "col"),), out_specs=P("row", ("col", "depth")), check_vma=False
    )
```

time: 366 us -> 104 us (0.28)
  the two profiles are of different devices: /device:TPU:1 before, /device:TPU:64 now
where the time goes in v3:
time: 104 us
  Pallas kernels  102 us (98%)
  local copies, waits for them, and re-layouts  2.02 us (2%)
    pallas_call x1, Pallas kernels, on_device(): pl.pallas_call(kernel, out_shape=jax.ShapeDtypeStruct((rows, share), F32)...  102 us

profile of v3, /device:TPU:64, one launch (start us, length us, event | category | flops | bytes accessed | tf_op | source)
XLA Modules:
  0.0 103.9 jit_solution(449647207750012040)
XLA Ops:
  0.0 0.0 copy-start
  0.0 1.2 %copy-done = bf16[512,1024]{1,0:T(8,128)(2,1)S(1)} copy-done((bf16[512,1024]{1,0:T(8,128)(2,1)S(1)}, bf16[512,1024]{1,0:T(8,128)(2,1)}, u32[]{:S(2)}) %copy-start) | copy-done | bytes 1048600
  1.2 101.9 %shard_map.17 = f32[512,256]{1,0:T(8,128)S(1)} custom-call(bf16[512,1024]{1,0:T(8,128)(2,1)S(1)} %copy-done), custom_call_target="tpu_custom_call" | custom-call | tf_op jit(solution)/shard_map/pallas_call | solution.py:432
  103.1 0.8 copy.3
Async XLA Ops:
  0.0 1.2 %copy-start = (bf16[512,1024]{1,0:T(8,128)(2,1)S(1)}, bf16[512,1024]{1,0:T(8,128)(2,1)}, u32[]{:S(2)}) copy-start(bf16[512,1024]{1,0:T(8,128)(2,1)} %a_hbm.1) | copy-start | bytes 3145732

commit v4 on v3

--- a/solution.py
+++ b/solution.py
@@ -18,8 +18,11 @@
 HOP = 5
 TICK = 0.75
 TICKS = 2 * UNITS + 4 * HOP
-PASS, COLLECT, RING, PERIOD = 4.1, 7.8, 3.5, 2.4
-PASS_CUBE, COLLECT_CUBE, PERIOD_CUBE = 5.5, 10.5, 4.5
+ROWS = [TICK * (s + 4 * HOP) for s in (STREAM // 2, STREAM, STREAM // 2, STREAM)]
+DOT = 0.4
+PASS, COLLECT, RING, PERIOD = (0.7, 0.7), (4.4, 4.4), 3.5, 2.4
+PASS_CUBE, NEAR_CUBE, COLLECT_CUBE, PERIOD_CUBE = 5.5, 10.0, 15.0, 2.0
+QUIET = 13.5
 
 
 def rem(a, b):
@@ -111,7 +114,7 @@
         u = div(n + 1, 3)
         others = lax.min(u, jnp.int32(1))
         g = others * (u - 1) + (1 - others) * n
-        e = others * (rem(n + 1, 3) + 1)
+        e = others * (rem(n, 3) + 1)
         at = pl.ds(pl.multiple_of(c * rows + k * unit, unit), unit)
         return bt.at[which, g, rem(x + gray(e), 4), at, :]
 
@@ -174,7 +177,7 @@
         for g in range(GROUPS):
             for k in range(SPLIT):
                 dst = bt.at[held, g, x, pl.ds(pl.multiple_of(core * rows + k * unit, unit), unit), :]
-                arrival = x_recv.at[(e + 1 + 3 * g) * SPLIT + k]
+                arrival = x_recv.at[(rem(e, 3) + 2 + 3 * g) * SPLIT + k]
                 start(own_piece(g, k), dst, x_send.at[g * SPLIT + k], arrival, (row, yh * 4 + to, yl))
 
     for d in range(2):
@@ -212,8 +215,8 @@
     sib_away = sib_w + 4 * (1 - lax.min(sib_w, jnp.int32(1)))
     sib_passed = rel_half(rem(z + 8 + (1 - 2 * core) * sib_away, 8), yh)
 
-    def arrived(g):
-        first, after = (0, 5 * SPLIT) if g == 0 else (5 * SPLIT, UNITS)
+    def arrived(g, b):
+        first, after = [n * SPLIT for n in ((0, 3), (3, 5), (5, 6), (6, 8))[2 * g + b]]
 
         @pl.loop(2 * first, 2 * after)
         def _(m):
@@ -225,7 +228,7 @@
 
         @pl.when(is_source)
         def _():
-            if g == 0:
+            if g == 0 and b == 0:
                 for i in range(2 * SPLIT):
                     own_copy(i // SPLIT, i % SPLIT).wait()
 
@@ -292,11 +295,14 @@
             n = (kind * 2 + d) * self.slots + self.slot(i)
             return self.sends.at[n], self.recvs.at[n]
 
-        def spread(self, i):
+        def spread_far(self, i):
             n = self.slot(i)
             for d in range(2):
                 src = self.part.at[self.at(across, i, d)]
                 send(src, self.relay.at[d, n], *self.sems(0, d, i), at_x(1 - 2 * d))
+
+        def spread_near(self, i):
+            n = self.slot(i)
             for d in range(2):
                 src = self.part.at[self.at(ahead if d == 0 else behind, i, 1 - d)]
                 send(src, self.raw.at[d, n], *self.sems(1, d, i), at_x(1 - 2 * d))
@@ -322,18 +328,14 @@
     square_sum = Sum(part1, relay1, raw1, summed1, rs1_send, rs1_recv, square_chunk)
     cube_sum = Sum(part2, relay2, raw2, summed2, rs2_send, rs2_recv, cube_chunk)
 
-    def multiply_square(g, r):
+    def multiply_square(g, r, b):
         at = pl.ds(r * square_chunk, square_chunk)
         left = jnp.concatenate([a_ref[at, :], other[at, :]], axis=1)
-
-        @pl.loop(0, 4, step=2)
-        def _(p):
-            right = jnp.concatenate(
-                [jnp.concatenate([bt[h, g, p], bt[h, g, p + 1]], axis=1) for h in range(2)], axis=0
-            )
-            product = jnp.dot(left, right, preferred_element_type=F32)
-            part1[g, p, at, :] = product[:, :cols]
-            part1[g, p + 1, at, :] = product[:, cols:]
+        p, q = rem(x + b, 4), rem(x + b + 2, 4)
+        right = jnp.concatenate([jnp.concatenate([bt[h, g, p], bt[h, g, q]], axis=1) for h in range(2)], axis=0)
+        product = jnp.dot(left, right, preferred_element_type=F32)
+        part1[g, p, at, :] = product[:, :cols]
+        part1[g, q, at, :] = product[:, cols:]
 
     def round_square(g, r):
         mid = square_chunk // 2
@@ -386,29 +388,37 @@
             own = jnp.concatenate([sb[g, yl, at, :] for g in range(GROUPS)], axis=1).astype(F32)
             out_ref[at, :] = 3.0 * own - 2.0 * total
 
-    events = []
+    events, square_sends = [], []
     last = {}
     for g in range(GROUPS):
-        begin = TICK * (2 * SPLIT * (5 if g == 0 else 8) + 4 * HOP)
+        begin, whole = [TICK * (2 * SPLIT * n + 4 * HOP) for n in ((3, 5), (6, 8))[g]]
+        events += [(begin, lambda g=g: arrived(g, 0)), (whole, lambda g=g: arrived(g, 1))]
         for r in range(SQUARE):
-            t = begin + r * PERIOD
-            if r == 0:
-                events.append((t, lambda g=g: arrived(g)))
+            t = max(begin, ROWS[r * 4 // SQUARE] if g == 0 else 0) + r * DOT
+            events.append((t, lambda g=g, r=r: (multiply_square(g, r, 0), square_sum.spread_far((g, r)))))
+            t = whole + r * PERIOD
             events += [
-                (t, lambda g=g, r=r: (multiply_square(g, r), square_sum.spread((g, r)))),
-                (t + PASS, lambda g=g, r=r: square_sum.pass_on((g, r))),
-                (t + COLLECT, lambda g=g, r=r: (round_square(g, r), gather(g, r, 0))),
+                (t, lambda g=g, r=r: multiply_square(g, r, 1)),
+                (t + PASS[g], lambda g=g, r=r: square_sum.pass_on((g, r))),
+                (t + PASS[g], lambda g=g, r=r: square_sum.spread_near((g, r))),
+                (t + COLLECT[g], lambda g=g, r=r: (round_square(g, r), gather(g, r, 0))),
             ]
             for s in range(1, 5):
-                events.append((t + COLLECT + RING * s, lambda g=g, r=r, s=s: gather(g, r, s)))
-            last[r] = t + COLLECT + RING * 4
+                events.append((t + COLLECT[g] + RING * s, lambda g=g, r=r, s=s: gather(g, r, s)))
+            last[r] = t + COLLECT[g] + RING * 4
     t = 0.0
     for r in range(CUBE):
-        t = max(t + PERIOD_CUBE, last[(r + 1) * SQUARE // CUBE - 1])
+        t = max(t + PERIOD, last[((r + 1) * SQUARE - 1) // CUBE])
+        if r == 0:
+            first = t
+            events.append((first + QUIET, lambda: finish_operands()))
+            events.append((first - 0.01, lambda: (square_sends.extend(sent), sent.clear())))
+            events.append((first + QUIET, lambda: [wait() for wait in square_sends]))
         events += [
-            (t, lambda r=r: (multiply_cube(r), cube_sum.spread((None, r)))),
+            (t, lambda r=r: (multiply_cube(r), cube_sum.spread_far((None, r)))),
             (t + PASS_CUBE, lambda r=r: cube_sum.pass_on((None, r))),
-            (t + COLLECT_CUBE, lambda r=r: purify(r)),
+            (t if r == 0 else first + NEAR_CUBE + r * PERIOD_CUBE, lambda r=r: cube_sum.spread_near((None, r))),
+            (first + COLLECT_CUBE + r * PERIOD_CUBE, lambda r=r: purify(r)),
         ]
     done = 0
     for t, event in sorted(events, key=lambda e: e[0]):
@@ -419,7 +429,6 @@
         event()
     for wait in sent:
         wait()
-    finish_operands()
 
 
 def on_device(density):

time: 104 us -> 98.5 us (0.947)
  the two profiles are of different devices: /device:TPU:64 before, /device:TPU:1 now
where the time goes in v4:
time: 98.5 us; the launch traced here: 98.3 us
  Pallas kernels  96.3 us (98%)
  local copies, waits for them, and re-layouts  2.02 us (2%)
    pallas_call x1, Pallas kernels, on_device(): pl.pallas_call(kernel, out_shape=jax.ShapeDtypeStruct((rows, share), F32)...  96.3 us
    unnamed x3, local copies, waits for them, and re-layouts  2.02 us

profile of v4, /device:TPU:1, one launch (start us, length us, event | category | flops | bytes accessed | tf_op | source)
XLA Modules:
  0.0 98.3 jit_solution(5956891740258513602)
XLA Ops:
  0.0 0.0 copy-start
  0.0 1.2 %copy-done = bf16[512,1024]{1,0:T(8,128)(2,1)S(1)} copy-done((bf16[512,1024]{1,0:T(8,128)(2,1)S(1)}, bf16[512,1024]{1,0:T(8,128)(2,1)}, u32[]{:S(2)}) %copy-start) | copy-done | bytes 1048600
  1.2 96.3 %shard_map.17 = f32[512,256]{1,0:T(8,128)S(1)} custom-call(bf16[512,1024]{1,0:T(8,128)(2,1)S(1)} %copy-done), custom_call_target="tpu_custom_call" | custom-call | tf_op jit(solution)/shard_map/pallas_call | solution.py:441
  97.5 0.8 copy.3
Async XLA Ops:
  0.0 1.2 %copy-start = (bf16[512,1024]{1,0:T(8,128)(2,1)S(1)}, bf16[512,1024]{1,0:T(8,128)(2,1)}, u32[]{:S(2)}) copy-start(bf16[512,1024]{1,0:T(8,128)(2,1)} %a_hbm.1) | copy-start | bytes 3145732

commit v5 on v4

--- a/solution.py
+++ b/solution.py
@@ -190,7 +190,7 @@
                 start(a_ref.at[at, :], other.at[at, :], y_send.at[n], y_recv.at[n], at_y(1 - 2 * d))
 
     def tick(t):
-        i = t
+        i = t - 3
 
         @pl.when(is_source & (i >= 2 * SPLIT) & (i < UNITS))
         def _():
@@ -198,7 +198,7 @@
             wait_recv(src, x_recv.at[i])
             inject(i, src)
 
-        m = t - HOP * away
+        m = t - 4 * away
 
         @pl.when((m >= 0) & (m < 2 * UNITS))
         def _():

time: 98.5 us -> 97.6 us (level)
  the two profiles are of different devices: /device:TPU:1 before, /device:TPU:24 now
where the time goes in v5:
time: 97.6 us; the launch traced here: 97.5 us
  Pallas kernels  95.4 us (98%)
  local copies, waits for them, and re-layouts  2.02 us (2%)
    pallas_call x1, Pallas kernels, on_device(): pl.pallas_call(kernel, out_shape=jax.ShapeDtypeStruct((rows, share), F32)...  95.4 us
    unnamed x3, local copies, waits for them, and re-layouts  2.02 us

profile of v5, /device:TPU:24, one launch (start us, length us, event | category | flops | bytes accessed | tf_op | source)
XLA Modules:
  0.0 97.5 jit_solution(7274778457918392467)
XLA Ops:
  0.0 0.0 copy-start
  0.0 1.2 %copy-done = bf16[512,1024]{1,0:T(8,128)(2,1)S(1)} copy-done((bf16[512,1024]{1,0:T(8,128)(2,1)S(1)}, bf16[512,1024]{1,0:T(8,128)(2,1)}, u32[]{:S(2)}) %copy-start) | copy-done | bytes 1048600
  1.2 95.4 %shard_map.17 = f32[512,256]{1,0:T(8,128)S(1)} custom-call(bf16[512,1024]{1,0:T(8,128)(2,1)S(1)} %copy-done), custom_call_target="tpu_custom_call" | custom-call | tf_op jit(solution)/shard_map/pallas_call | solution.py:441
  96.7 0.8 copy.3
Async XLA Ops:
  0.0 1.2 %copy-start = (bf16[512,1024]{1,0:T(8,128)(2,1)S(1)}, bf16[512,1024]{1,0:T(8,128)(2,1)}, u32[]{:S(2)}) copy-start(bf16[512,1024]{1,0:T(8,128)(2,1)} %a_hbm.1) | copy-start | bytes 3145732

commit v6 on v5

--- a/solution.py
+++ b/solution.py
@@ -190,6 +190,19 @@
                 start(a_ref.at[at, :], other.at[at, :], y_send.at[n], y_recv.at[n], at_y(1 - 2 * d))
 
     def tick(t):
+        m = t - 4 * away
+
+        @pl.when((m >= 0) & (m < 2 * UNITS))
+        def _():
+            ring(m)
+
+        for d in range(2):
+            j = t - HOP * (yl + 1 if d == 0 else 4 - yl)
+
+            @pl.when((j >= 0) & (j < STREAM))
+            def _():
+                stream(d, j)
+
         i = t - 3
 
         @pl.when(is_source & (i >= 2 * SPLIT) & (i < UNITS))
@@ -197,19 +210,6 @@
             src = tile(held, i, core)
             wait_recv(src, x_recv.at[i])
             inject(i, src)
-
-        m = t - 4 * away
-
-        @pl.when((m >= 0) & (m < 2 * UNITS))
-        def _():
-            ring(m)
-
-        for d in range(2):
-            j = t - HOP * (yl + 1 if d == 0 else 4 - yl)
-
-            @pl.when((j >= 0) & (j < STREAM))
-            def _():
-                stream(d, j)
 
     sib_w = rem(4 - w, 4)
     sib_away = sib_w + 4 * (1 - lax.min(sib_w, jnp.int32(1)))

time: 97.6 us -> 97.6 us (level)
  no operation moved by 1% of the time
where the time goes in v6:
time: 97.6 us; the launch traced here: 97.4 us
  Pallas kernels  95.4 us (98%)
  local copies, waits for them, and re-layouts  2.02 us (2%)
    pallas_call x1, Pallas kernels, on_device(): pl.pallas_call(kernel, out_shape=jax.ShapeDtypeStruct((rows, share), F32)...  95.4 us
    unnamed x3, local copies, waits for them, and re-layouts  2.02 us

profile of v6, /device:TPU:24, one launch (start us, length us, event | category | flops | bytes accessed | tf_op | source)
XLA Modules:
  0.0 97.4 jit_solution(2774994845857724607)
XLA Ops:
  0.0 0.0 copy-start
  0.0 1.2 %copy-done = bf16[512,1024]{1,0:T(8,128)(2,1)S(1)} copy-done((bf16[512,1024]{1,0:T(8,128)(2,1)S(1)}, bf16[512,1024]{1,0:T(8,128)(2,1)}, u32[]{:S(2)}) %copy-start) | copy-done | bytes 1048600
  1.2 95.4 %shard_map.17 = f32[512,256]{1,0:T(8,128)S(1)} custom-call(bf16[512,1024]{1,0:T(8,128)(2,1)S(1)} %copy-done), custom_call_target="tpu_custom_call" | custom-call | tf_op jit(solution)/shard_map/pallas_call | solution.py:441
  96.6 0.8 copy.3
Async XLA Ops:
  0.0 1.2 %copy-start = (bf16[512,1024]{1,0:T(8,128)(2,1)S(1)}, bf16[512,1024]{1,0:T(8,128)(2,1)}, u32[]{:S(2)}) copy-start(bf16[512,1024]{1,0:T(8,128)(2,1)} %a_hbm.1) | copy-start | bytes 3145732
